TPU v7x, 32 devices: a whole 2x2x4 slice. The times are simulated.
32 devices in a mesh: seq: 16 (over z, x, core), dp: 2 (over y).
Axes of the slice: x: 2, y: 2, z: 4, core: 2. Of those that a mesh axis runs over, the one named last changes fastest.
Arguments:
- queries: bfloat16 [2, 1024, 2048], P(None, 'seq', 'dp'), may hold values from -10 to 10
- key_rows: bfloat16 [2, 1024, 2048], P(None, 'seq', 'dp'), may hold values from -10 to 10
- value_rows: bfloat16 [2, 1024, 2048], P(None, 'seq', 'dp'), may hold values from -6 to 6
- query_tangent: bfloat16 [2, 1024, 2048], P(None, 'seq', 'dp'), may hold values from -6 to 6
- key_tangent: bfloat16 [2, 1024, 2048], P(None, 'seq', 'dp'), may hold values from -6 to 6
- out_adjoint: bfloat16 [2, 1024, 2048], P(None, 'seq', 'dp'), may hold values from -6 to 6
Outputs:
- query_product: bfloat16 [2, 1024, 2048], P(None, 'seq', 'dp')
- key_product: bfloat16 [2, 1024, 2048], P(None, 'seq', 'dp')
- value_product: bfloat16 [2, 1024, 2048], P(None, 'seq', 'dp')
- curvature: float32 [2, 16], replicated
All inputs are finite; a program needn't handle non-finite values.
Results may differ from a plain program's by a relative error of at most 0.0051.
Values may be sent and summed in bfloat16 or wider, within the bound.
A program may use at most 64 MiB of HBM per device.

v0:
```python
import functools
import math

import jax
import jax.numpy as jnp
from jax import lax
from jax.experimental import pallas as pl
from jax.experimental.pallas import tpu as pltpu
from jax.sharding import PartitionSpec as P

HEAD_DIM = 128
ROWS = 256
SLOTS = 3
MESH = pl.DeviceIdType.MESH
F32 = jnp.float32
BF16 = jnp.bfloat16


def mm(left, right, dims):
    return lax.dot_general(left, right, (dims, ((), ())), preferred_element_type=F32)


def kernel(
    n,
    m,
    local_heads,
    q_in,
    k_in,
    v_in,
    tq_in,
    tk_in,
    g_in,
    q_out,
    k_out,
    v_out,
    curv_out,
    qq,
    kk,
    gg,
    vv,
    hk_acc,
    hv_acc,
    q_staged,
    k_staged,
    v_staged,
    k_low,
    v_low,
    mine,
    board,
    in_send,
    in_recv,
    out_send,
    out_recv,
    low_recv,
    board_send,
    board_recv,
):
    D = HEAD_DIM
    me = lax.axis_index("seq")
    dp = lax.axis_index("dp")
    tokens = q_in.shape[1]
    quarter = n // 4
    half = n // 2
    length = n * tokens
    upper = half * tokens
    rows = min(ROWS, upper)
    per_block = rows // tokens
    factor = D ** (-0.5)
    level = me // quarter
    ring = me % quarter
    near = 1 - level % 2
    low = level < 2
    slots = 1 + (SLOTS - 1) * near

    barrier = pltpu.get_barrier_semaphore()

    def greet(step, carry):
        other = lax.rem(dp * n + me + step, n * m)
        pl.semaphore_signal(
            barrier, inc=1, device_id=(other % n, other // n), device_id_type=MESH
        )
        return carry

    lax.fori_loop(1, n * m, greet, 0)

    tensors = (
        (k_in, kk, 0, length),
        (tk_in, kk, D, length),
        (v_in, vv, 0, length),
        (q_in, qq, D, upper),
        (tq_in, qq, 0, upper),
        (g_in, gg, 0, upper),
    )

    def columns(pair):
        return pl.ds(pl.multiple_of((pair % local_heads) * D, D), D)

    def feed(number, pair, slot, home, row):
        source, buf, column, span = tensors[number]
        src = source.at[pair // local_heads, :, columns(pair)]
        at = pl.multiple_of(slot * span + row, tokens)
        dst = buf.at[pl.ds(at, tokens), column : column + D]

        @pl.when(home == me)
        def _():
            pltpu.make_async_copy(src, dst, in_recv.at[slot, number]).start()

        @pl.when(home != me)
        def _():
            pltpu.make_async_remote_copy(
                src_ref=src,
                dst_ref=dst,
                send_sem=in_send.at[number],
                recv_sem=in_recv.at[slot, number],
                device_id=(home, dp),
                device_id_type=MESH,
            ).start()

    pl.semaphore_wait(barrier, n * m - 1)

    for group in (0, 3, 1, 2):
        far = 1 if group == 3 else 0
        slot = 0 if far else group

        def send(step, carry, group=group, far=far, slot=slot):
            spot = (me + step) % quarter
            pair = group * quarter + spot
            low_home = far * quarter + spot
            high_home = half + far * quarter + spot

            @pl.when(low)
            def _():
                for number in range(6):
                    feed(number, pair, slot, low_home, me * tokens)
                for number in range(3):
                    feed(number, pair, slot, high_home, me * tokens)

            @pl.when(jnp.logical_not(low))
            def _():
                for number in range(3):
                    feed(number, pair, slot, high_home, me * tokens)
                for number in range(3, 6):
                    feed(number, pair, slot, high_home, (me - half) * tokens)

            return carry

        lax.fori_loop(0, quarter, send, 0)

    shape = mine.shape
    mine[...] = jnp.zeros(shape, F32)

    def ship(staged, at, other, dst, number, recv):
        src = staged.at[pl.ds(pl.multiple_of(at, tokens), tokens), :]

        @pl.when(other == me)
        def _():
            pltpu.make_async_copy(src, dst, recv).start()

        @pl.when(other != me)
        def _():
            pltpu.make_async_remote_copy(
                src_ref=src,
                dst_ref=dst,
                send_sem=out_send.at[number],
                recv_sem=recv,
                device_id=(other, dp),
                device_id_type=MESH,
            ).start()

    def work(slot, base):
        group = near * slot + (1 - near) * 3
        pair = group * quarter + ring
        batch = pair // local_heads
        cols = columns(pair)
        keys = base + upper
        top_rows = pl.multiple_of(slot * upper, rows)
        top_keys = pl.multiple_of(slot * length, rows)

        def arrived(number, count):
            _, buf, column, span = tensors[number]
            whole = buf.at[:count, column : column + D]
            pltpu.make_async_copy(whole, whole, in_recv.at[slot, number]).wait()

        for number in range(6):
            arrived(number, keys if number < 3 else upper)

        kappa = jnp.zeros((1, 1), F32)
        for start in reversed(range(base, keys, rows)):
            width = start + rows
            here = pl.ds(pl.multiple_of(top_rows + (start - base), rows), rows)
            seen = pl.ds(top_keys, width)
            both = qq[here, :]
            adj = gg[here, :]
            both_keys = kk[seen, :]
            scores = mm(both[:, D:], both_keys[:, :D], ((1,), (1,)))
            row = lax.broadcasted_iota(jnp.int32, (rows, width), 0) + start
            col = lax.broadcasted_iota(jnp.int32, (rows, width), 1)
            scores = jnp.where(row >= col, scores, -jnp.inf)
            top = jnp.max(scores, axis=1, keepdims=True)
            weights = jnp.exp2((scores - top) * (factor * math.log2(math.e)))
            probs = weights * (1.0 / jnp.sum(weights, axis=1, keepdims=True))
            tangent = factor * mm(both, both_keys, ((1,), (1,)))
            mean = jnp.sum(probs * tangent, axis=1, keepdims=True)
            tprobs = probs * (tangent - mean)
            gprobs = mm(adj, vv[seen, :], ((1,), (1,)))
            delta = jnp.sum(probs * gprobs, axis=1, keepdims=True)
            centered = gprobs - delta
            tdelta = jnp.sum(tprobs * gprobs, axis=1, keepdims=True)
            tprob_low = tprobs.astype(BF16)
            gscore_low = (probs * centered).astype(BF16)
            second_low = (tprobs * centered - probs * tdelta).astype(BF16)
            hv = mm(tprob_low, adj, ((0,), (0,)))
            hq = factor * (
                mm(second_low, both_keys[:, :D], ((1,), (0,)))
                + mm(gscore_low, both_keys[:, D:], ((1,), (0,)))
            )
            hk = factor * (
                mm(second_low, both[:, D:], ((0,), (0,)))
                + mm(gscore_low, both[:, :D], ((0,), (0,)))
            )
            if width == keys:
                hk_acc[:keys, :] = hk
                hv_acc[:keys, :] = hv
            else:
                hk_acc[:width, :] += hk
                hv_acc[:width, :] += hv
            kappa += jnp.sum(both[:, :D].astype(F32) * hq, keepdims=True)
            q_staged[here, :] = hq.astype(BF16)

            done = start if start > base else 0
            count = width - done
            span = slice(done, width)
            area = pl.ds(pl.multiple_of(top_keys + done, rows), count)
            hk_done = hk_acc[span, :]
            kappa += jnp.sum(kk[area, D:].astype(F32) * hk_done, keepdims=True)
            k_staged[area, :] = hk_done.astype(BF16)
            v_staged[area, :] = hv_acc[span, :].astype(BF16)

            def give_q(step, carry, start=start):
                other = start // tokens + step
                at = top_rows + other * tokens - base
                ship(q_staged, at, other, q_out.at[batch, :, cols], 0, out_recv.at[0])
                return carry

            def give_kv(step, carry, done=done):
                other = done // tokens + step
                at = top_keys + other * tokens
                if base:
                    ship(k_staged, at, other, k_out.at[batch, :, cols], 1, out_recv.at[1])
                    ship(v_staged, at, other, v_out.at[batch, :, cols], 2, out_recv.at[2])
                else:
                    ship(k_staged, at, other, k_low.at[batch, :, cols], 1, low_recv.at[0])
                    ship(v_staged, at, other, v_low.at[batch, :, cols], 2, low_recv.at[1])
                return carry

            lax.fori_loop(0, count // tokens, give_kv, 0)
            lax.fori_loop(0, per_block, give_q, 0)

        at_row = lax.broadcasted_iota(jnp.int32, shape, 0) == batch
        at_col = (
            lax.broadcasted_iota(jnp.int32, shape, 1) == dp * local_heads + pair % local_heads
        )
        mine[...] += jnp.where(jnp.logical_and(at_row, at_col), kappa, 0.0)

    def all_slots(base):
        def one(slot, carry):
            work(slot, base)
            return carry

        lax.fori_loop(0, slots, one, 0)

    @pl.when(low)
    def _():
        all_slots(0)

    @pl.when(jnp.logical_not(low))
    def _():
        all_slots(upper)

    place = dp * n + me

    def tell(step, carry):
        other = (place + step) % (n * m)
        pltpu.make_async_remote_copy(
            src_ref=mine,
            dst_ref=board.at[place],
            send_sem=board_send,
            recv_sem=board_recv,
            device_id=(other % n, other // n),
            device_id_type=MESH,
        ).start()
        return carry

    pltpu.make_async_copy(mine, board.at[place], board_recv).start()
    lax.fori_loop(1, n * m, tell, 0)

    def gone(units, sem):
        sent = vv.at[: units * tokens, :]
        pltpu.make_async_copy(sent, sent, sem).wait()

    for is_low in (True, False):
        for count, is_near in ((SLOTS, 1), (1, 0)):

            @pl.when(jnp.logical_and(low == is_low, near == is_near))
            def _(is_low=is_low, count=count):
                for number in range(6):
                    gone(n - count + (n if is_low and number < 3 else 0), in_send.at[number])
                gone(count * (half - 1), out_send.at[0])
                for number in (1, 2):
                    gone(count * ((half if is_low else n) - 1), out_send.at[number])

    sent = board.at[: n * m - 1]
    pltpu.make_async_copy(sent, sent, board_send).wait()

    pltpu.make_async_copy(q_out, q_out, out_recv.at[0]).wait()
    pltpu.make_async_copy(k_out, k_out, out_recv.at[1]).wait()
    pltpu.make_async_copy(v_out, v_out, out_recv.at[2]).wait()

    @pl.when(low)
    def _():
        pltpu.make_async_copy(k_low, k_low, low_recv.at[0]).wait()
        pltpu.make_async_copy(v_low, v_low, low_recv.at[1]).wait()
        k_out[...] = (k_out[...].astype(F32) + k_low[...].astype(F32)).astype(BF16)
        v_out[...] = (v_out[...].astype(F32) + v_low[...].astype(F32)).astype(BF16)

    pltpu.make_async_copy(board, board, board_recv).wait()
    total = jnp.sum(board[...], axis=0)
    curv_out[...] = total[: curv_out.shape[0], : curv_out.shape[1]]


def local(n, m, queries, key_rows, value_rows, query_tangent, key_tangent, out_adjoint):
    batch, tokens, width = queries.shape
    local_heads = width // HEAD_DIM
    length = n * tokens
    heads = local_heads * m
    board_shape = (-(-batch // 8) * 8, -(-heads // 128) * 128)
    result = jax.ShapeDtypeStruct(queries.shape, BF16)
    D = HEAD_DIM
    return pl.pallas_call(
        functools.partial(kernel, n, m, local_heads),
        out_shape=(result, result, result, jax.ShapeDtypeStruct((batch, heads), F32)),
        in_specs=[pl.BlockSpec(memory_space=pl.ANY)] * 6,
        out_specs=(pl.BlockSpec(memory_space=pltpu.VMEM),) * 4,
        scratch_shapes=[
            pltpu.VMEM((SLOTS * length // 2, 2 * D), BF16),
            pltpu.VMEM((SLOTS * length, 2 * D), BF16),
            pltpu.VMEM((SLOTS * length // 2, D), BF16),
            pltpu.VMEM((SLOTS * length, D), BF16),
            pltpu.VMEM((length, D), F32),
            pltpu.VMEM((length, D), F32),
            pltpu.VMEM((SLOTS * length // 2, D), BF16),
            pltpu.VMEM((SLOTS * length, D), BF16),
            pltpu.VMEM((SLOTS * length, D), BF16),
            pltpu.VMEM(queries.shape, BF16),
            pltpu.VMEM(queries.shape, BF16),
            pltpu.VMEM(board_shape, F32),
            pltpu.VMEM((n * m,) + board_shape, F32),
            pltpu.SemaphoreType.DMA((6,)),
            pltpu.SemaphoreType.DMA((SLOTS, 6)),
            pltpu.SemaphoreType.DMA((3,)),
            pltpu.SemaphoreType.DMA((3,)),
            pltpu.SemaphoreType.DMA((2,)),
            pltpu.SemaphoreType.DMA,
            pltpu.SemaphoreType.DMA,
        ],
        compiler_params=pltpu.CompilerParams(
            collective_id=0, has_side_effects=True, vmem_limit_bytes=56 * 1024 * 1024
        ),
    )(queries, key_rows, value_rows, query_tangent, key_tangent, out_adjoint)


def solution(mesh):
    split = P(None, "seq", "dp")
    return jax.shard_map(
        functools.partial(local, mesh.shape["seq"], mesh.shape["dp"]),
        mesh=mesh,
        in_specs=(split,) * 6,
        out_specs=(split, split, split, P()),
        check_vma=False,
    )
```

profile of v0, /device:TPU:0, one launch (start us, length us, event | category | flops | bytes accessed | tf_op | source)
XLA Modules:
  0.0 67.6 jit_solution(1802469988388234576)
XLA Ops:
  0.6 63.0 %shard_map.93 = (bf16[2,64,1024]{2,1,0:T(8,128)(2,1)}, bf16[2,64,1024]{2,1,0:T(8,128)(2,1)}, bf16[2,64,1024]{2,1,0:T(8,128)(2,1)}, f32[2,16]{1,0:T(2,128)}) custom-call(bf16[2,64,1024]{2,1,0:T(8,128)(2,1)} %q_in.1, bf16[2,64,1024]{2,1,0:T(8,128)(2,1)} %k_in.1, bf16[2,64,1024]{2,1,0:T(8,128)(2,1)} %v_in.1, bf16[2,64,1024]{2,1,0:T(8,128)(2,1)} %tq_in.1, ...), custom_call_target="tpu_custom_call" | custom-call | tf_op jit(solution)/shard_map/pallas_call | solution.py:339
  63.6 0.0 copy-start.1
  63.6 1.7 %copy.14 = bf16[2,64,1024]{2,1,0:T(8,128)(2,1)} copy(bf16[2,64,1024]{2,1,0:T(8,128)(2,1)} %get-tuple-element.8) | data formatting | bytes 524288
  65.3 0.0 copy-done.1
  65.3 0.0 copy-start
  65.3 0.7 %copy.15 = bf16[2,64,1024]{2,1,0:T(8,128)(2,1)} copy(bf16[2,64,1024]{2,1,0:T(8,128)(2,1)S(1)} %copy-done.1) | data formatting | bytes 524288
  66.0 0.3 copy-done
  66.4 0.0 copy-start.2
  66.4 0.7 %copy.16 = bf16[2,64,1024]{2,1,0:T(8,128)(2,1)} copy(bf16[2,64,1024]{2,1,0:T(8,128)(2,1)S(1)} %copy-done) | data formatting | bytes 524288
  67.1 0.0 copy-done.2
  67.1 0.6 copy.17
Async XLA Ops:
  63.6 1.7 %copy-start.1 = (bf16[2,64,1024]{2,1,0:T(8,128)(2,1)S(1)}, bf16[2,64,1024]{2,1,0:T(8,128)(2,1)}, u32[]{:S(2)}) copy-start(bf16[2,64,1024]{2,1,0:T(8,128)(2,1)} %get-tuple-element.9) | copy-start | bytes 786436
  65.3 1.0 %copy-start = (bf16[2,64,1024]{2,1,0:T(8,128)(2,1)S(1)}, bf16[2,64,1024]{2,1,0:T(8,128)(2,1)}, u32[]{:S(2)}) copy-start(bf16[2,64,1024]{2,1,0:T(8,128)(2,1)} %get-tuple-element.10) | copy-start | bytes 786436
  66.4 0.7 %copy-start.2 = (f32[2,16]{1,0:T(2,128)S(1)}, f32[2,16]{1,0:T(2,128)}, u32[]{:S(2)}) copy-start(f32[2,16]{1,0:T(2,128)} %get-tuple-element.11) | copy-start | bytes 388
where the time goes:
time: 67.8 us; the launch traced here: 67.6 us
  Pallas kernels  63 us (93%)
  local copies, waits for them, and re-layouts  4.03 us (6%)
    pallas_call x1, Pallas kernels, local(): pl.pallas_call(functools.partial(kernel, n, m, local_heads), out_shape=(r...  63 us
    unnamed x10, local copies, waits for them, and re-layouts  4.03 us

commit v1 on v0

v1 whole, which is shorter than its diff:
```python
import functools
import math

import jax
import jax.numpy as jnp
from jax import lax
from jax.experimental import pallas as pl
from jax.experimental.pallas import tpu as pltpu
from jax.sharding import PartitionSpec as P

HEAD_DIM = 128
MESH = pl.DeviceIdType.MESH
F32 = jnp.float32
BF16 = jnp.bfloat16
KEYS = (0, 1, 2)
QUERIES = (3, 4, 5)


def mm(left, right, dims):
    return lax.dot_general(left, right, (dims, ((), ())), preferred_element_type=F32)


def kernel(
    n,
    m,
    local_heads,
    q_in,
    k_in,
    v_in,
    tq_in,
    tk_in,
    g_in,
    q_out,
    k_out,
    v_out,
    curv_out,
    qq,
    kk,
    gg,
    vv,
    hk_acc,
    hv_acc,
    q_staged,
    k_staged,
    v_staged,
    q_low,
    k_low,
    v_low,
    stat_out,
    stat_in,
    mine,
    board,
    x_send,
    x_recv,
    z_send,
    z_recv,
    stat_send,
    stat_recv,
    out_send,
    out_recv,
    low_recv,
    board_send,
    board_recv,
    reach,
):
    D = HEAD_DIM
    me = lax.axis_index("seq")
    dp = lax.axis_index("dp")
    tokens = q_in.shape[1]
    batches = q_in.shape[0]
    quarter = n // 4
    block = quarter * tokens
    factor = D ** (-0.5)
    level = me // quarter
    ring = me % quarter
    place = dp * n + me

    barrier = pltpu.get_barrier_semaphore()

    def hail(sem, seq, row):
        pl.semaphore_signal(sem, inc=1, device_id=(seq, row), device_id_type=MESH)

    def level_mate(step):
        return level * quarter + (ring + step) % quarter

    def column_mate(step):
        return (me + step * quarter) % n

    def greet_level(step, carry):
        hail(barrier, level_mate(step), dp)
        return carry

    def greet_rows(step, carry):
        hail(barrier, me, (dp + step) % m)
        return carry

    for step in range(1, 4):
        hail(barrier, column_mate(step), dp)
    lax.fori_loop(1, quarter, greet_level, 0)
    lax.fori_loop(1, m, greet_rows, 0)
    pl.semaphore_wait(barrier, quarter - 1 + 3 + m - 1)

    tensors = (
        (k_in, kk, 0),
        (tk_in, kk, D),
        (v_in, vv, 0),
        (q_in, qq, D),
        (tq_in, qq, 0),
        (g_in, gg, 0),
    )

    def columns(pair):
        return pl.ds(pl.multiple_of((pair % local_heads) * D, D), D)

    def rows_of(group, index, count=1):
        return slice((group * 4 + index) * block, (group * 4 + index + count) * block)

    def program(here):
        x_waited = set()
        z_waited = set()
        started = set()
        sent = {"z": 0, "stat": 0, "out": 0}
        kappas = {}

        def spread(group, number):
            source, buf, column = tensors[number]
            base = (group * 4 + here) * block
            at = pl.multiple_of(base + ring * tokens, tokens)
            dst = buf.at[pl.ds(at, tokens), column : column + D]
            sem = x_recv.at[group * 6 + number]

            def src(pair):
                return source.at[pair // local_heads, :, columns(pair)]

            def send(step, carry):
                spot = (ring + step) % quarter
                pltpu.make_async_remote_copy(
                    src_ref=src(group * quarter + spot),
                    dst_ref=dst,
                    send_sem=x_send,
                    recv_sem=sem,
                    device_id=(here * quarter + spot, dp),
                    device_id_type=MESH,
                ).start()
                return carry

            pltpu.make_async_copy(src(group * quarter + ring), dst, sem).start()
            lax.fori_loop(1, quarter, send, 0)

        def x_wait(group, number):
            if (group, number) in x_waited:
                return
            x_waited.add((group, number))
            _, buf, column = tensors[number]
            whole = buf.at[rows_of(group, here), column : column + D]
            pltpu.make_async_copy(whole, whole, x_recv.at[group * 6 + number]).wait()

        def relay(group, side, there):
            for number in side:
                x_wait(group, number)
                _, buf, column = tensors[number]
                part = buf.at[rows_of(group, here), column : column + D]
                pltpu.make_async_remote_copy(
                    src_ref=part,
                    dst_ref=part,
                    send_sem=z_send,
                    recv_sem=z_recv.at[(group * 4 + here) * 2 + side[0] // 3],
                    device_id=(there * quarter + ring, dp),
                    device_id_type=MESH,
                ).start()
                sent["z"] += 1

        def need(group, index, side):
            if index == here:
                for number in side:
                    x_wait(group, number)
            elif (group, index, side[0]) not in z_waited:
                z_waited.add((group, index, side[0]))
                whole = vv.at[: 3 * block, :]
                sem = z_recv.at[(group * 4 + index) * 2 + side[0] // 3]
                pltpu.make_async_copy(whole, whole, sem).wait()

        def first(group, index, low, high):
            need(group, index, QUERIES)
            for key in range(low, high):
                need(group, key, KEYS)
            both = qq[rows_of(group, index), :]
            adj = gg[rows_of(group, index), :]
            keys = rows_of(group, low, high - low)
            both_keys = kk[keys, :]
            size = (high - low) * block
            scores = mm(both_keys[:, :D], both[:, D:], ((1,), (1,)))
            if high == index + 1:
                key = lax.broadcasted_iota(jnp.int32, (size, block), 0) + low * block
                row = lax.broadcasted_iota(jnp.int32, (size, block), 1) + index * block
                scores = jnp.where(row >= key, scores, -jnp.inf)
            top = jnp.max(scores, axis=0, keepdims=True)
            weights = jnp.exp2((scores - top) * (factor * math.log2(math.e)))
            tangent = factor * mm(both_keys, both, ((1,), (1,)))
            gprobs = mm(vv[keys, :], adj, ((1,), (1,)))
            moved = weights * tangent
            stats = (
                top,
                jnp.sum(weights, axis=0, keepdims=True),
                jnp.sum(moved, axis=0, keepdims=True),
                jnp.sum(weights * gprobs, axis=0, keepdims=True),
                jnp.sum(moved * gprobs, axis=0, keepdims=True),
            )
            return (weights, tangent, gprobs), stats

        def tell(group, index, stats, there):
            slot = group * 4 + index
            stat_out[slot] = jnp.concatenate(stats + stats[:3], axis=0)
            pltpu.make_async_remote_copy(
                src_ref=stat_out.at[slot],
                dst_ref=stat_in.at[slot],
                send_sem=stat_send,
                recv_sem=stat_recv.at[slot],
                device_id=(there * quarter + ring, dp),
                device_id_type=MESH,
            ).start()
            sent["stat"] += 1

        def merged(group, index, stats):
            slot = group * 4 + index
            pltpu.make_async_copy(stat_in.at[slot], stat_in.at[slot], stat_recv.at[slot]).wait()
            other = stat_in[slot]
            top = jnp.maximum(stats[0], other[0:1, :])
            power = factor * math.log2(math.e)
            ours = jnp.exp2((stats[0] - top) * power)
            theirs = jnp.exp2((other[0:1, :] - top) * power)
            sums = [ours * stats[k] + theirs * other[k : k + 1, :] for k in range(1, 5)]
            return ours, sums

        def second(group, index, low, high, arrays, scale, sums):
            weights, tangent, gprobs = arrays
            over = 1.0 / sums[0]
            mean = sums[1] * over
            delta = sums[2] * over
            tdelta = sums[3] * over - mean * delta
            probs = weights * (over if scale is None else scale * over)
            tprobs = probs * (tangent - mean)
            centered = gprobs - delta
            tprob_low = tprobs.astype(BF16)
            gscore_low = (probs * centered).astype(BF16)
            second_low = (tprobs * centered - probs * tdelta).astype(BF16)
            both = qq[rows_of(group, index), :]
            adj = gg[rows_of(group, index), :]
            both_keys = kk[rows_of(group, low, high - low), :]
            hv = mm(tprob_low, adj, ((1,), (0,)))
            hk = factor * (
                mm(second_low, both[:, D:], ((1,), (0,)))
                + mm(gscore_low, both[:, :D], ((1,), (0,)))
            )
            hq = factor * (
                mm(second_low, both_keys[:, :D], ((0,), (0,)))
                + mm(gscore_low, both_keys[:, D:], ((0,), (0,)))
            )
            for key in range(low, high):
                area = rows_of(group, key)
                part = slice((key - low) * block, (key - low + 1) * block)
                if (group, key) in started:
                    hk_acc[area, :] += hk[part, :]
                    hv_acc[area, :] += hv[part, :]
                else:
                    started.add((group, key))
                    hk_acc[area, :] = hk[part, :]
                    hv_acc[area, :] = hv[part, :]
            owe(group, jnp.sum(both[:, :D].astype(F32) * hq, axis=0, keepdims=True))
            q_staged[rows_of(group, index), :] = hq.astype(BF16)
            ship(group, index, ((q_staged, q_out, q_low, 0),))

        def owe(group, value):
            kappas[group] = kappas[group] + value if group in kappas else value

        def ship(group, index, results):
            pair = group * quarter + ring
            batch = pair // local_heads
            cols = columns(pair)
            base = (group * 4 + index) * block
            home = index == here

            def give(step, carry):
                spot = (ring + step) % quarter
                at = pl.multiple_of(base + spot * tokens, tokens)
                for staged, out, far, number in results:
                    pltpu.make_async_remote_copy(
                        src_ref=staged.at[pl.ds(at, tokens), :],
                        dst_ref=(out if home else far).at[batch, :, cols],
                        send_sem=out_send,
                        recv_sem=(out_recv if home else low_recv).at[number],
                        device_id=(index * quarter + spot, dp),
                        device_id_type=MESH,
                    ).start()
                return carry

            if home:
                at = pl.multiple_of(base + ring * tokens, tokens)
                for staged, out, _, number in results:
                    pltpu.make_async_copy(
                        staged.at[pl.ds(at, tokens), :], out.at[batch, :, cols], out_recv.at[number]
                    ).start()
            lax.fori_loop(1 if home else 0, quarter, give, 0)
            sent["out"] += (quarter - (1 if home else 0)) * len(results)

        def finish(group, index):
            area = rows_of(group, index)
            hk = hk_acc[area, :]
            k_staged[area, :] = hk.astype(BF16)
            v_staged[area, :] = hv_acc[area, :].astype(BF16)
            ship(group, index, ((k_staged, k_out, k_low, 1), (v_staged, v_out, v_low, 2)))
            owe(group, jnp.sum(kk[area, D:].astype(F32) * hk, axis=0, keepdims=True))

        def whole(group, index, low, high):
            arrays, stats = first(group, index, low, high)
            second(group, index, low, high, arrays, None, stats[1:])

        def early(group, index, low, high, there):
            arrays, stats = first(group, index, low, high)
            tell(group, index, stats, there)
            return arrays, stats

        def later(group, index, low, high, held):
            arrays, stats = held
            ours, sums = merged(group, index, stats)
            second(group, index, low, high, arrays, ours, sums)

        def both_ways(group, index, low, high, there):
            later(group, index, low, high, early(group, index, low, high, there))

        def spread_all(order):
            for group, side in order:
                for number in side:
                    spread(group, number)

        def meet():
            pl.semaphore_wait(reach.at[0], 3)
            lax.fori_loop(
                1, m, lambda step, carry: (hail(reach.at[1], me, (dp + step) % m), carry)[1], 0
            )

        K, Q = KEYS, QUERIES
        orders = (
            ((0, K), (2, K), (1, K), (3, K), (0, Q), (2, Q), (1, Q), (3, Q)),
            ((0, K), (0, Q), (1, K), (1, Q), (2, Q), (2, K), (3, Q), (3, K)),
            ((2, Q), (2, K), (3, Q), (3, K), (0, K), (0, Q), (1, K), (1, Q)),
            ((2, Q), (0, Q), (0, K), (2, K), (3, Q), (1, Q), (1, K), (3, K)),
        )
        spread_all(orders[here])
        for step in range(1, 4):
            hail(reach.at[0], column_mate(step), dp)

        if here == 0:
            relay(0, K, 2)
            relay(2, K, 1)
            relay(1, K, 2)
            relay(3, K, 1)
            meet()
            for near, far in ((0, 2), (1, 3)):
                both_ways(near, 1, 0, 1, 1)
                whole(near, 0, 0, 1)
                finish(near, 0)
                whole(far, 0, 0, 1)
                finish(far, 0)
        elif here == 1:
            relay(0, K, 2)
            relay(0, Q, 0)
            relay(1, K, 2)
            relay(1, Q, 0)
            meet()
            held = [early(group, 1, 1, 2, 0) for group in (0, 1)]
            for near, far in ((0, 2), (1, 3)):
                both_ways(far, 2, 0, 2, 2)
                both_ways(far, 3, 0, 2, 3)
                whole(far, 1, 0, 2)
                finish(far, 0)
                finish(far, 1)
                later(near, 1, 1, 2, held[near])
                finish(near, 1)
        elif here == 2:
            relay(2, Q, 1)
            relay(2, K, 3)
            relay(3, Q, 1)
            relay(3, K, 3)
            meet()
            held = [early(group, 2, 2, 3, 1) for group in (2, 3)]
            for near, far in ((0, 2), (1, 3)):
                both_ways(near, 3, 0, 3, 3)
                whole(near, 2, 0, 3)
                finish(near, 0)
                finish(near, 1)
                finish(near, 2)
                later(far, 2, 2, 3, held[near])
                finish(far, 2)
        else:
            relay(2, Q, 1)
            relay(0, Q, 2)
            held = {0: early(0, 3, 3, 4, 2)}
            relay(3, Q, 1)
            relay(1, Q, 2)
            meet()
            held[2] = early(2, 3, 2, 4, 1)
            held[1] = early(1, 3, 3, 4, 2)
            held[3] = early(3, 3, 2, 4, 1)
            for near, far in ((0, 2), (1, 3)):
                later(far, 3, 2, 4, held[far])
                finish(far, 2)
                finish(far, 3)
                later(near, 3, 3, 4, held[near])
                finish(near, 3)

        shape = mine.shape
        total = jnp.zeros(shape, F32)
        row = lax.broadcasted_iota(jnp.int32, shape, 0)
        col = lax.broadcasted_iota(jnp.int32, shape, 1)
        for group in range(4):
            pair = group * quarter + ring
            at_row = row == pair // local_heads
            at_col = col == dp * local_heads + pair % local_heads
            kappa = jnp.sum(kappas[group], keepdims=True)
            total += jnp.where(jnp.logical_and(at_row, at_col), kappa, 0.0)
        mine[...] = total

        pl.semaphore_wait(reach.at[1], m - 1)

        def post(step, carry):
            other = (place + step) % (n * m)
            pltpu.make_async_remote_copy(
                src_ref=mine,
                dst_ref=board.at[place],
                send_sem=board_send,
                recv_sem=board_recv,
                device_id=(other % n, other // n),
                device_id_type=MESH,
            ).start()
            return carry

        pltpu.make_async_copy(mine, board.at[place], board_recv).start()
        lax.fori_loop(1, n * m, post, 0)

        def drain(count, sem):
            part = qq.at[: count // 2, :]
            pltpu.make_async_copy(part, part, sem).wait()

        drain(24 * (quarter - 1) * tokens, x_send)
        drain(sent["z"] * block, z_send)
        stats_sent = stat_out.at[: sent["stat"]]
        pltpu.make_async_copy(stats_sent, stats_sent, stat_send).wait()
        drain(sent["out"] * tokens, out_send)

        middle = batches // 2
        near_half, far_half, full = slice(0, middle), slice(middle, batches), slice(0, batches)
        spans = ((None, full), (near_half, near_half), (far_half, far_half), (full, None))[here]
        targets = ((q_out, q_low), (k_out, k_low), (v_out, v_low))
        for number, span in enumerate((spans[0], spans[1], spans[1])):
            out, far = targets[number]
            pltpu.make_async_copy(out, out, out_recv.at[number]).wait()
            if span is not None:
                extra = far.at[span]
                pltpu.make_async_copy(extra, extra, low_recv.at[number]).wait()
                out[span] = (out[span].astype(F32) + far[span].astype(F32)).astype(BF16)

    for here in range(4):
        pl.when(level == here)(functools.partial(program, here))

    sent = board.at[: n * m - 1]
    pltpu.make_async_copy(sent, sent, board_send).wait()
    pltpu.make_async_copy(board, board, board_recv).wait()
    total = jnp.sum(board[...], axis=0)
    curv_out[...] = total[: curv_out.shape[0], : curv_out.shape[1]]


def local(n, m, queries, key_rows, value_rows, query_tangent, key_tangent, out_adjoint):
    batch, tokens, width = queries.shape
    local_heads = width // HEAD_DIM
    block = n // 4 * tokens
    rows = 16 * block
    heads = local_heads * m
    board_shape = (-(-batch // 8) * 8, -(-heads // 128) * 128)
    result = jax.ShapeDtypeStruct(queries.shape, BF16)
    D = HEAD_DIM
    return pl.pallas_call(
        functools.partial(kernel, n, m, local_heads),
        out_shape=(result, result, result, jax.ShapeDtypeStruct((batch, heads), F32)),
        in_specs=[pl.BlockSpec(memory_space=pl.ANY)] * 6,
        out_specs=(pl.BlockSpec(memory_space=pltpu.VMEM),) * 4,
        scratch_shapes=[
            pltpu.VMEM((rows, 2 * D), BF16),
            pltpu.VMEM((rows, 2 * D), BF16),
            pltpu.VMEM((rows, D), BF16),
            pltpu.VMEM((rows, D), BF16),
            pltpu.VMEM((rows, D), F32),
            pltpu.VMEM((rows, D), F32),
            pltpu.VMEM((rows, D), BF16),
            pltpu.VMEM((rows, D), BF16),
            pltpu.VMEM((rows, D), BF16),
            pltpu.VMEM(queries.shape, BF16),
            pltpu.VMEM(queries.shape, BF16),
            pltpu.VMEM(queries.shape, BF16),
            pltpu.VMEM((16, 8, block), F32),
            pltpu.VMEM((16, 8, block), F32),
            pltpu.VMEM(board_shape, F32),
            pltpu.VMEM((n * m,) + board_shape, F32),
            pltpu.SemaphoreType.DMA,
            pltpu.SemaphoreType.DMA((24,)),
            pltpu.SemaphoreType.DMA,
            pltpu.SemaphoreType.DMA((32,)),
            pltpu.SemaphoreType.DMA,
            pltpu.SemaphoreType.DMA((16,)),
            pltpu.SemaphoreType.DMA,
            pltpu.SemaphoreType.DMA((3,)),
            pltpu.SemaphoreType.DMA((3,)),
            pltpu.SemaphoreType.DMA,
            pltpu.SemaphoreType.DMA,
            pltpu.SemaphoreType.REGULAR((2,)),
        ],
        compiler_params=pltpu.CompilerParams(
            collective_id=0, has_side_effects=True, vmem_limit_bytes=56 * 1024 * 1024
        ),
    )(queries, key_rows, value_rows, query_tangent, key_tangent, out_adjoint)


def solution(mesh):
    split = P(None, "seq", "dp")
    return jax.shard_map(
        functools.partial(local, mesh.shape["seq"], mesh.shape["dp"]),
        mesh=mesh,
        in_specs=(split,) * 6,
        out_specs=(split, split, split, P()),
        check_vma=False,
    )
```

time: 67.8 us -> 50.7 us (0.75)
  Pallas kernels: 63 us -> 45.8 us
    pallas_call x1, Pallas kernels: 63 us -> 45.8 us  [local(): pl.pallas_call(functools.partial(kernel, n, m, local_heads), out_shape=(r...]
where the time goes in v1:
time: 50.7 us; the launch traced here: 50.5 us
  Pallas kernels  45.8 us (90%)
  local copies, waits for them, and re-layouts  4.03 us (8%)
  between operations  0.65 us (1%)
    pallas_call x1, Pallas kernels, local(): pl.pallas_call(functools.partial(kernel, n, m, local_heads), out_shape=(r...  45.8 us
    unnamed x10, local copies, waits for them, and re-layouts  4.03 us

profile of v1, /device:TPU:0, one launch (start us, length us, event | category | flops | bytes accessed | tf_op | source)
XLA Modules:
  0.0 50.5 jit_solution(14573063477769290808)
XLA Ops:
  0.6 45.8 %shard_map.93 = (bf16[2,64,1024]{2,1,0:T(8,128)(2,1)}, bf16[2,64,1024]{2,1,0:T(8,128)(2,1)}, bf16[2,64,1024]{2,1,0:T(8,128)(2,1)}, f32[2,16]{1,0:T(2,128)}) custom-call(bf16[2,64,1024]{2,1,0:T(8,128)(2,1)} %q_in.1, bf16[2,64,1024]{2,1,0:T(8,128)(2,1)} %k_in.1, bf16[2,64,1024]{2,1,0:T(8,128)(2,1)} %v_in.1, bf16[2,64,1024]{2,1,0:T(8,128)(2,1)} %tq_in.1, ...), custom_call_target="tpu_custom_call" | custom-call | tf_op jit(solution)/shard_map/pallas_call | solution.py:482
  46.5 0.0 copy-start.1
  46.5 1.7 %copy.14 = bf16[2,64,1024]{2,1,0:T(8,128)(2,1)} copy(bf16[2,64,1024]{2,1,0:T(8,128)(2,1)} %get-tuple-element.8) | data formatting | bytes 524288
  48.2 0.0 copy-done.1
  48.2 0.0 copy-start
  48.2 0.7 %copy.15 = bf16[2,64,1024]{2,1,0:T(8,128)(2,1)} copy(bf16[2,64,1024]{2,1,0:T(8,128)(2,1)S(1)} %copy-done.1) | data formatting | bytes 524288
  48.9 0.3 copy-done
  49.3 0.0 copy-start.2
  49.3 0.7 %copy.16 = bf16[2,64,1024]{2,1,0:T(8,128)(2,1)} copy(bf16[2,64,1024]{2,1,0:T(8,128)(2,1)S(1)} %copy-done) | data formatting | bytes 524288
  50.0 0.0 copy-done.2
  50.0 0.6 %copy.17 = f32[2,16]{1,0:T(2,128)} copy(f32[2,16]{1,0:T(2,128)S(1)} %copy-done.2) | data formatting | bytes 256
Async XLA Ops:
  46.5 1.7 %copy-start.1 = (bf16[2,64,1024]{2,1,0:T(8,128)(2,1)S(1)}, bf16[2,64,1024]{2,1,0:T(8,128)(2,1)}, u32[]{:S(2)}) copy-start(bf16[2,64,1024]{2,1,0:T(8,128)(2,1)} %get-tuple-element.9) | copy-start | bytes 786436
  48.2 1.0 %copy-start = (bf16[2,64,1024]{2,1,0:T(8,128)(2,1)S(1)}, bf16[2,64,1024]{2,1,0:T(8,128)(2,1)}, u32[]{:S(2)}) copy-start(bf16[2,64,1024]{2,1,0:T(8,128)(2,1)} %get-tuple-element.10) | copy-start | bytes 786436
  49.3 0.7 %copy-start.2 = (f32[2,16]{1,0:T(2,128)S(1)}, f32[2,16]{1,0:T(2,128)}, u32[]{:S(2)}) copy-start(f32[2,16]{1,0:T(2,128)} %get-tuple-element.11) | copy-start | bytes 388

commit v2 on v1

--- a/solution.py
+++ b/solution.py
@@ -33,6 +33,9 @@
     q_out,
     k_out,
     v_out,
+    q_low,
+    k_low,
+    v_low,
     curv_out,
     qq,
     kk,
@@ -43,13 +46,12 @@
     q_staged,
     k_staged,
     v_staged,
-    q_low,
-    k_low,
-    v_low,
     stat_out,
     stat_in,
     mine,
-    board,
+    by_level,
+    by_ring,
+    by_row,
     x_send,
     x_recv,
     z_send,
@@ -73,7 +75,6 @@
     factor = D ** (-0.5)
     level = me // quarter
     ring = me % quarter
-    place = dp * n + me
 
     barrier = pltpu.get_barrier_semaphore()
 
@@ -334,10 +335,7 @@
                     spread(group, number)
 
         def meet():
-            pl.semaphore_wait(reach.at[0], 3)
-            lax.fori_loop(
-                1, m, lambda step, carry: (hail(reach.at[1], me, (dp + step) % m), carry)[1], 0
-            )
+            pl.semaphore_wait(reach, 3)
 
         K, Q = KEYS, QUERIES
         orders = (
@@ -348,7 +346,7 @@
         )
         spread_all(orders[here])
         for step in range(1, 4):
-            hail(reach.at[0], column_mate(step), dp)
+            hail(reach, column_mate(step), dp)
 
         if here == 0:
             relay(0, K, 2)
@@ -421,22 +419,50 @@
             total += jnp.where(jnp.logical_and(at_row, at_col), kappa, 0.0)
         mine[...] = total
 
-        pl.semaphore_wait(reach.at[1], m - 1)
-
-        def post(step, carry):
-            other = (place + step) % (n * m)
+        def post(dst, sem, seq, row):
             pltpu.make_async_remote_copy(
                 src_ref=mine,
-                dst_ref=board.at[place],
+                dst_ref=dst,
                 send_sem=board_send,
-                recv_sem=board_recv,
-                device_id=(other % n, other // n),
+                recv_sem=board_recv.at[sem],
+                device_id=(seq, row),
                 device_id_type=MESH,
             ).start()
-            return carry
-
-        pltpu.make_async_copy(mine, board.at[place], board_recv).start()
-        lax.fori_loop(1, n * m, post, 0)
+
+        def gather(buf, own, count, sem):
+            arrivals = buf.at[:count]
+            pltpu.make_async_copy(arrivals, arrivals, board_recv.at[sem]).wait()
+            buf[own] = mine[...]
+            return jnp.sum(buf[...], axis=0)
+
+        def gone(count):
+            part = by_ring.at[:count]
+            pltpu.make_async_copy(part, part, board_send).wait()
+
+        if here < 3:
+            post(by_level.at[here], 0, 3 * quarter + ring, dp)
+            gone(1)
+        else:
+            mine[...] = gather(by_level, 3, 3, 0)
+
+            def post_ring(step, carry):
+                post(by_ring.at[ring], 1, level_mate(step), dp)
+                return carry
+
+            def post_row(step, carry):
+                post(by_row.at[dp], 2, me, (dp + step) % m)
+                return carry
+
+            lax.fori_loop(1, quarter, post_ring, 0)
+            gone(quarter - 1)
+            mine[...] = gather(by_ring, ring, quarter - 1, 1)
+            lax.fori_loop(1, m, post_row, 0)
+            gone(m - 1)
+            mine[...] = gather(by_row, dp, m - 1, 2)
+            curv_out[...] = mine[...]
+            for there in range(3):
+                post(curv_out, 3, there * quarter + ring, dp)
+            gone(3)
 
         def drain(count, sem):
             part = qq.at[: count // 2, :]
@@ -448,26 +474,72 @@
         pltpu.make_async_copy(stats_sent, stats_sent, stat_send).wait()
         drain(sent["out"] * tokens, out_send)
 
-        middle = batches // 2
-        near_half, far_half, full = slice(0, middle), slice(middle, batches), slice(0, batches)
-        spans = ((None, full), (near_half, near_half), (far_half, far_half), (full, None))[here]
-        targets = ((q_out, q_low), (k_out, k_low), (v_out, v_low))
-        for number, span in enumerate((spans[0], spans[1], spans[1])):
-            out, far = targets[number]
+        low_spans = spans_of(here, batches)
+        arrivals = ((q_out, q_low), (k_out, k_low), (v_out, v_low))
+        for number, (out, far) in enumerate(arrivals):
             pltpu.make_async_copy(out, out, out_recv.at[number]).wait()
-            if span is not None:
-                extra = far.at[span]
+            if low_spans[number] is not None:
+                extra = far.at[low_spans[number]]
                 pltpu.make_async_copy(extra, extra, low_recv.at[number]).wait()
-                out[span] = (out[span].astype(F32) + far[span].astype(F32)).astype(BF16)
+        if here < 3:
+            pltpu.make_async_copy(curv_out, curv_out, board_recv.at[3]).wait()
 
     for here in range(4):
         pl.when(level == here)(functools.partial(program, here))
 
-    sent = board.at[: n * m - 1]
-    pltpu.make_async_copy(sent, sent, board_send).wait()
-    pltpu.make_async_copy(board, board, board_recv).wait()
-    total = jnp.sum(board[...], axis=0)
-    curv_out[...] = total[: curv_out.shape[0], : curv_out.shape[1]]
+
+def spans_of(here, batches):
+    middle = batches // 2
+    near, far, every = slice(0, middle), slice(middle, batches), slice(0, batches)
+    keys, queries = (every, near, far, None)[here], (None, near, far, every)[here]
+    return queries, keys, keys
+
+
+def merge_kernel(n, *refs):
+    homes, lows, curv_in = refs[0:3], refs[3:6], refs[6]
+    outs, curv_out = refs[7:10], refs[10]
+    home_bufs, low_bufs, curv_buf, curv_small = refs[11:14], refs[14:17], refs[17], refs[18]
+    in_sems, low_sems, out_sems = refs[19:22]
+    level = lax.axis_index("seq") // (n // 4)
+    batches = homes[0].shape[0]
+    loads = [pltpu.make_async_copy(homes[k], home_bufs[k], in_sems.at[k]) for k in range(3)]
+    loads.append(pltpu.make_async_copy(curv_in, curv_buf, in_sems.at[3]))
+    stores = [pltpu.make_async_copy(home_bufs[k], outs[k], out_sems.at[k]) for k in range(3)]
+    stores.append(pltpu.make_async_copy(curv_small, curv_out, out_sems.at[3]))
+
+    def extra(here, number):
+        span = spans_of(here, batches)[number]
+        return span, None if span is None else pltpu.make_async_copy(
+            lows[number].at[span], low_bufs[number].at[span], low_sems.at[number]
+        )
+
+    def fetch(here):
+        for number in range(3):
+            span, copy = extra(here, number)
+            if span is not None:
+                copy.start()
+
+    def add(here):
+        for number in range(3):
+            loads[number].wait()
+            span, copy = extra(here, number)
+            if span is not None:
+                copy.wait()
+                total = home_bufs[number][span].astype(F32) + low_bufs[number][span].astype(F32)
+                home_bufs[number][span] = total.astype(BF16)
+            stores[number].start()
+
+    for copy in loads:
+        copy.start()
+    for here in range(4):
+        pl.when(level == here)(functools.partial(fetch, here))
+    loads[3].wait()
+    curv_small[...] = curv_buf[: curv_small.shape[0], : curv_small.shape[1]]
+    stores[3].start()
+    for here in range(4):
+        pl.when(level == here)(functools.partial(add, here))
+    for copy in stores:
+        copy.wait()
 
 
 def local(n, m, queries, key_rows, value_rows, query_tangent, key_tangent, out_adjoint):
@@ -479,11 +551,12 @@
     board_shape = (-(-batch // 8) * 8, -(-heads // 128) * 128)
     result = jax.ShapeDtypeStruct(queries.shape, BF16)
     D = HEAD_DIM
-    return pl.pallas_call(
+    anywhere = pl.BlockSpec(memory_space=pl.ANY)
+    *parts, curvature = pl.pallas_call(
         functools.partial(kernel, n, m, local_heads),
-        out_shape=(result, result, result, jax.ShapeDtypeStruct((batch, heads), F32)),
-        in_specs=[pl.BlockSpec(memory_space=pl.ANY)] * 6,
-        out_specs=(pl.BlockSpec(memory_space=pltpu.VMEM),) * 4,
+        out_shape=(result,) * 6 + (jax.ShapeDtypeStruct(board_shape, F32),),
+        in_specs=[anywhere] * 6,
+        out_specs=(anywhere,) * 6 + (pl.BlockSpec(memory_space=pltpu.VMEM),),
         scratch_shapes=[
             pltpu.VMEM((rows, 2 * D), BF16),
             pltpu.VMEM((rows, 2 * D), BF16),
@@ -494,13 +567,12 @@
             pltpu.VMEM((rows, D), BF16),
             pltpu.VMEM((rows, D), BF16),
             pltpu.VMEM((rows, D), BF16),
-            pltpu.VMEM(queries.shape, BF16),
-            pltpu.VMEM(queries.shape, BF16),
-            pltpu.VMEM(queries.shape, BF16),
             pltpu.VMEM((16, 8, block), F32),
             pltpu.VMEM((16, 8, block), F32),
             pltpu.VMEM(board_shape, F32),
-            pltpu.VMEM((n * m,) + board_shape, F32),
+            pltpu.VMEM((4,) + board_shape, F32),
+            pltpu.VMEM((n // 4,) + board_shape, F32),
+            pltpu.VMEM((m,) + board_shape, F32),
             pltpu.SemaphoreType.DMA,
             pltpu.SemaphoreType.DMA((24,)),
             pltpu.SemaphoreType.DMA,
@@ -511,13 +583,28 @@
             pltpu.SemaphoreType.DMA((3,)),
             pltpu.SemaphoreType.DMA((3,)),
             pltpu.SemaphoreType.DMA,
-            pltpu.SemaphoreType.DMA,
-            pltpu.SemaphoreType.REGULAR((2,)),
+            pltpu.SemaphoreType.DMA((4,)),
+            pltpu.SemaphoreType.REGULAR,
         ],
         compiler_params=pltpu.CompilerParams(
             collective_id=0, has_side_effects=True, vmem_limit_bytes=56 * 1024 * 1024
         ),
     )(queries, key_rows, value_rows, query_tangent, key_tangent, out_adjoint)
+
+    return pl.pallas_call(
+        functools.partial(merge_kernel, n),
+        out_shape=(result, result, result, jax.ShapeDtypeStruct((batch, heads), F32)),
+        in_specs=[anywhere] * 7,
+        out_specs=(anywhere,) * 4,
+        scratch_shapes=[pltpu.VMEM(queries.shape, BF16)] * 6
+        + [
+            pltpu.VMEM(board_shape, F32),
+            pltpu.VMEM((batch, heads), F32),
+            pltpu.SemaphoreType.DMA((4,)),
+            pltpu.SemaphoreType.DMA((3,)),
+            pltpu.SemaphoreType.DMA((4,)),
+        ],
+    )(*parts, curvature)
 
 
 def solution(mesh):

time: 50.7 us -> 53.6 us (1.057)
  Pallas kernels: 45.8 us -> 52.6 us
  local copies, waits for them, and re-layouts: 4.03 us -> 0 us
    pallas_call x1, Pallas kernels: 45.8 us -> 50.5 us  [local(): pl.pallas_call(functools.partial(kernel, n, m, local_heads), out_shape=(r...]
    unnamed x10 -> x0, local copies, waits for them, and re-layouts: 4.03 us -> none
    pallas_call x0 -> x1, Pallas kernels: none -> 2.14 us  [local(): pl.pallas_call(functools.partial(merge_kernel, n), out_shape=(result, res...]
where the time goes in v2:
time: 53.6 us; the launch traced here: 53.5 us
  Pallas kernels  52.6 us (98%)
  between operations  0.84 us (2%)
    pallas_call x1, Pallas kernels, local(): pl.pallas_call(functools.partial(kernel, n, m, local_heads), out_shape=(r...  50.5 us
    pallas_call x1, Pallas kernels, local(): pl.pallas_call(functools.partial(merge_kernel, n), out_shape=(result, res...  2.14 us

profile of v2, /device:TPU:0, one launch (start us, length us, event | category | flops | bytes accessed | tf_op | source)
XLA Modules:
  0.0 53.5 jit_solution(15363937436438763032)
XLA Ops:
  0.6 50.5 %shard_map.93 = (bf16[2,64,1024]{2,1,0:T(8,128)(2,1)}, bf16[2,64,1024]{2,1,0:T(8,128)(2,1)}, bf16[2,64,1024]{2,1,0:T(8,128)(2,1)}, bf16[2,64,1024]{2,1,0:T(8,128...) custom-call(bf16[2,64,1024]{2,1,0:T(8,128)(2,1)} %q_in.1, ...), custom_call_target="tpu_custom_call" | custom-call | tf_op jit(solution)/shard_map/pallas_call | solution.py:555
  51.1 2.1 %shard_map.94 = (bf16[2,64,1024]{2,1,0:T(8,128)(2,1)}, bf16[2,64,1024]{2,1,0:T(8,128)(2,1)}, bf16[2,64,1024]{2,1,0:T(8,128)(2,1)}, f32[2,16]{1,0:T(2,128)}) custom-call(bf16[2,64,1024]{2,1,0:T(8,128)(2,1)} %get-tuple-element.11.refs_0_, bf16[2,64,1024]{2,1,0:T(8,128)(2,1)} %get-tuple-element.12.refs_1_, bf16[2,64,1024]{2,1,0:T(8,128)(2,1)} %get-tuple-element.13.refs_2_, ...), custom_call_target="tpu_custom_call" | custom-call | tf_op jit(solution)/shard_map/pallas_call | solution.py:594

commit v3 on v2

--- a/solution.py
+++ b/solution.py
@@ -49,9 +49,7 @@
     stat_out,
     stat_in,
     mine,
-    by_level,
-    by_ring,
-    by_row,
+    board,
     x_send,
     x_recv,
     z_send,
@@ -75,6 +73,7 @@
     factor = D ** (-0.5)
     level = me // quarter
     ring = me % quarter
+    place = dp * n + me
 
     barrier = pltpu.get_barrier_semaphore()
 
@@ -83,9 +82,6 @@
 
     def level_mate(step):
         return level * quarter + (ring + step) % quarter
-
-    def column_mate(step):
-        return (me + step * quarter) % n
 
     def greet_level(step, carry):
         hail(barrier, level_mate(step), dp)
@@ -95,11 +91,14 @@
         hail(barrier, me, (dp + step) % m)
         return carry
 
-    for step in range(1, 4):
-        hail(barrier, column_mate(step), dp)
+    def greet_mates(step, carry):
+        hail(reach.at[0], me, (dp + step) % m)
+        return carry
+
     lax.fori_loop(1, quarter, greet_level, 0)
     lax.fori_loop(1, m, greet_rows, 0)
-    pl.semaphore_wait(barrier, quarter - 1 + 3 + m - 1)
+    pl.semaphore_wait(barrier, quarter - 1 + m - 1 + (level + 3) // 4)
+    pl.when(level < 3)(lambda: hail(barrier, me + quarter, dp))
 
     tensors = (
         (k_in, kk, 0),
@@ -120,6 +119,7 @@
         x_waited = set()
         z_waited = set()
         started = set()
+        entered = set()
         sent = {"z": 0, "stat": 0, "out": 0}
         kappas = {}
 
@@ -157,6 +157,7 @@
             pltpu.make_async_copy(whole, whole, x_recv.at[group * 6 + number]).wait()
 
         def relay(group, side, there):
+            known(there)
             for number in side:
                 x_wait(group, number)
                 _, buf, column = tensors[number]
@@ -210,6 +211,7 @@
             return (weights, tangent, gprobs), stats
 
         def tell(group, index, stats, there):
+            known(there)
             slot = group * 4 + index
             stat_out[slot] = jnp.concatenate(stats + stats[:3], axis=0)
             pltpu.make_async_remote_copy(
@@ -233,7 +235,7 @@
             sums = [ours * stats[k] + theirs * other[k : k + 1, :] for k in range(1, 5)]
             return ours, sums
 
-        def second(group, index, low, high, arrays, scale, sums):
+        def second(group, index, low, high, arrays, scale, sums, now=True):
             weights, tangent, gprobs = arrays
             over = 1.0 / sums[0]
             mean = sums[1] * over
@@ -269,6 +271,10 @@
                     hv_acc[area, :] = hv[part, :]
             owe(group, jnp.sum(both[:, :D].astype(F32) * hq, axis=0, keepdims=True))
             q_staged[rows_of(group, index), :] = hq.astype(BF16)
+            if now:
+                give_queries(group, index)
+
+        def give_queries(group, index):
             ship(group, index, ((q_staged, q_out, q_low, 0),))
 
         def owe(group, value):
@@ -321,91 +327,126 @@
             tell(group, index, stats, there)
             return arrays, stats
 
-        def later(group, index, low, high, held):
+        def later(group, index, low, high, held, now=True):
             arrays, stats = held
             ours, sums = merged(group, index, stats)
-            second(group, index, low, high, arrays, ours, sums)
-
-        def both_ways(group, index, low, high, there):
-            later(group, index, low, high, early(group, index, low, high, there))
-
-        def spread_all(order):
+            second(group, index, low, high, arrays, ours, sums, now)
+
+        def both_ways(group, index, low, high, there, now=True):
+            later(group, index, low, high, early(group, index, low, high, there), now)
+
+        def spread_all(*order):
             for group, side in order:
                 for number in side:
                     spread(group, number)
 
         def meet():
-            pl.semaphore_wait(reach, 3)
+            for there in range(here + 1, 4):
+                known(there)
+            lax.fori_loop(1, m, greet_mates, 0)
+
+        def known(there):
+            if there > here and there not in entered:
+                entered.add(there)
+                pl.semaphore_wait(reach.at[there], 1)
 
         K, Q = KEYS, QUERIES
-        orders = (
-            ((0, K), (2, K), (1, K), (3, K), (0, Q), (2, Q), (1, Q), (3, Q)),
-            ((0, K), (0, Q), (1, K), (1, Q), (2, Q), (2, K), (3, Q), (3, K)),
-            ((2, Q), (2, K), (3, Q), (3, K), (0, K), (0, Q), (1, K), (1, Q)),
-            ((2, Q), (0, Q), (0, K), (2, K), (3, Q), (1, Q), (1, K), (3, K)),
-        )
-        spread_all(orders[here])
-        for step in range(1, 4):
-            hail(reach, column_mate(step), dp)
+        for below in range(here):
+            hail(reach.at[here], below * quarter + ring, dp)
 
         if here == 0:
+            spread_all((2, K), (0, K), (3, K))
+            relay(2, K, 1)
             relay(0, K, 2)
-            relay(2, K, 1)
+            spread_all((1, K), (0, Q), (2, Q), (1, Q), (3, Q))
+            relay(3, K, 1)
             relay(1, K, 2)
-            relay(3, K, 1)
             meet()
-            for near, far in ((0, 2), (1, 3)):
-                both_ways(near, 1, 0, 1, 1)
-                whole(near, 0, 0, 1)
-                finish(near, 0)
-                whole(far, 0, 0, 1)
-                finish(far, 0)
+            both_ways(0, 1, 0, 1, 1)
+            whole(0, 0, 0, 1)
+            finish(0, 0)
+            for group in (2, 3):
+                whole(group, 0, 0, 1)
+                finish(group, 0)
+            both_ways(1, 1, 0, 1, 1)
+            whole(1, 0, 0, 1)
+            finish(1, 0)
         elif here == 1:
+            spread_all((0, K), (0, Q), (2, Q))
             relay(0, K, 2)
+            spread_all((2, K), (1, K))
             relay(0, Q, 0)
+            spread_all((1, Q), (3, Q), (3, K))
+            held = {0: early(0, 1, 1, 2, 0)}
+            meet()
+            front = early(2, 2, 0, 2, 2)
             relay(1, K, 2)
             relay(1, Q, 0)
-            meet()
-            held = [early(group, 1, 1, 2, 0) for group in (0, 1)]
-            for near, far in ((0, 2), (1, 3)):
-                both_ways(far, 2, 0, 2, 2)
-                both_ways(far, 3, 0, 2, 3)
-                whole(far, 1, 0, 2)
-                finish(far, 0)
-                finish(far, 1)
-                later(near, 1, 1, 2, held[near])
-                finish(near, 1)
+            held[1] = early(1, 1, 1, 2, 0)
+            back = early(2, 3, 0, 2, 3)
+            later(2, 2, 0, 2, front, False)
+            later(2, 3, 0, 2, back, False)
+            whole(2, 1, 0, 2)
+            finish(2, 0)
+            finish(2, 1)
+            later(0, 1, 1, 2, held[0])
+            finish(0, 1)
+            front = early(3, 2, 0, 2, 2)
+            back = early(3, 3, 0, 2, 3)
+            later(3, 2, 0, 2, front, False)
+            later(3, 3, 0, 2, back, False)
+            for group in (2, 3):
+                give_queries(group, 2)
+                give_queries(group, 3)
+            whole(3, 1, 0, 2)
+            finish(3, 0)
+            finish(3, 1)
+            later(1, 1, 1, 2, held[1])
+            finish(1, 1)
         elif here == 2:
+            spread_all((2, Q), (2, K), (0, K))
             relay(2, Q, 1)
+            spread_all((0, Q), (3, Q))
             relay(2, K, 3)
+            spread_all((3, K), (1, K), (1, Q))
+            held = {2: early(2, 2, 2, 3, 1)}
             relay(3, Q, 1)
             relay(3, K, 3)
             meet()
-            held = [early(group, 2, 2, 3, 1) for group in (2, 3)]
-            for near, far in ((0, 2), (1, 3)):
-                both_ways(near, 3, 0, 3, 3)
-                whole(near, 2, 0, 3)
-                finish(near, 0)
-                finish(near, 1)
-                finish(near, 2)
-                later(far, 2, 2, 3, held[near])
-                finish(far, 2)
+            held[3] = early(3, 2, 2, 3, 1)
+            both_ways(0, 3, 0, 3, 3)
+            whole(0, 2, 0, 3)
+            finish(0, 0)
+            finish(0, 1)
+            finish(0, 2)
+            later(2, 2, 2, 3, held[2])
+            finish(2, 2)
+            both_ways(1, 3, 0, 3, 3)
+            whole(1, 2, 0, 3)
+            finish(1, 0)
+            finish(1, 1)
+            finish(1, 2)
+            later(3, 2, 2, 3, held[3])
+            finish(3, 2)
         else:
+            spread_all((0, Q), (2, Q), (0, K))
+            relay(0, Q, 2)
+            spread_all((2, K), (1, Q))
             relay(2, Q, 1)
-            relay(0, Q, 2)
+            spread_all((1, K), (3, Q), (3, K))
             held = {0: early(0, 3, 3, 4, 2)}
-            relay(3, Q, 1)
-            relay(1, Q, 2)
             meet()
             held[2] = early(2, 3, 2, 4, 1)
+            relay(1, Q, 2)
             held[1] = early(1, 3, 3, 4, 2)
+            relay(3, Q, 1)
             held[3] = early(3, 3, 2, 4, 1)
-            for near, far in ((0, 2), (1, 3)):
-                later(far, 3, 2, 4, held[far])
-                finish(far, 2)
-                finish(far, 3)
-                later(near, 3, 3, 4, held[near])
-                finish(near, 3)
+            for group in (0, 1):
+                later(group, 3, 3, 4, held[group])
+                finish(group, 3)
+                later(group + 2, 3, 2, 4, held[group + 2])
+                finish(group + 2, 2)
+                finish(group + 2, 3)
 
         shape = mine.shape
         total = jnp.zeros(shape, F32)
@@ -413,56 +454,28 @@
         col = lax.broadcasted_iota(jnp.int32, shape, 1)
         for group in range(4):
             pair = group * quarter + ring
-            at_row = row == pair // local_heads
-            at_col = col == dp * local_heads + pair % local_heads
+            spot = (pair // local_heads) * (local_heads * m) + dp * local_heads + pair % local_heads
+            at_row = row == spot // 128
+            at_col = col == spot % 128
             kappa = jnp.sum(kappas[group], keepdims=True)
             total += jnp.where(jnp.logical_and(at_row, at_col), kappa, 0.0)
         mine[...] = total
-
-        def post(dst, sem, seq, row):
+        pl.semaphore_wait(reach.at[0], m - 1)
+
+        def post(step, carry):
+            other = (place + step) % (n * m)
             pltpu.make_async_remote_copy(
                 src_ref=mine,
-                dst_ref=dst,
+                dst_ref=board.at[place],
                 send_sem=board_send,
-                recv_sem=board_recv.at[sem],
-                device_id=(seq, row),
+                recv_sem=board_recv,
+                device_id=(other % n, other // n),
                 device_id_type=MESH,
             ).start()
-
-        def gather(buf, own, count, sem):
-            arrivals = buf.at[:count]
-            pltpu.make_async_copy(arrivals, arrivals, board_recv.at[sem]).wait()
-            buf[own] = mine[...]
-            return jnp.sum(buf[...], axis=0)
-
-        def gone(count):
-            part = by_ring.at[:count]
-            pltpu.make_async_copy(part, part, board_send).wait()
-
-        if here < 3:
-            post(by_level.at[here], 0, 3 * quarter + ring, dp)
-            gone(1)
-        else:
-            mine[...] = gather(by_level, 3, 3, 0)
-
-            def post_ring(step, carry):
-                post(by_ring.at[ring], 1, level_mate(step), dp)
-                return carry
-
-            def post_row(step, carry):
-                post(by_row.at[dp], 2, me, (dp + step) % m)
-                return carry
-
-            lax.fori_loop(1, quarter, post_ring, 0)
-            gone(quarter - 1)
-            mine[...] = gather(by_ring, ring, quarter - 1, 1)
-            lax.fori_loop(1, m, post_row, 0)
-            gone(m - 1)
-            mine[...] = gather(by_row, dp, m - 1, 2)
-            curv_out[...] = mine[...]
-            for there in range(3):
-                post(curv_out, 3, there * quarter + ring, dp)
-            gone(3)
+            return carry
+
+        pltpu.make_async_copy(mine, board.at[place], board_recv).start()
+        lax.fori_loop(1, n * m, post, 0)
 
         def drain(count, sem):
             part = qq.at[: count // 2, :]
@@ -481,11 +494,14 @@
             if low_spans[number] is not None:
                 extra = far.at[low_spans[number]]
                 pltpu.make_async_copy(extra, extra, low_recv.at[number]).wait()
-        if here < 3:
-            pltpu.make_async_copy(curv_out, curv_out, board_recv.at[3]).wait()
 
     for here in range(4):
         pl.when(level == here)(functools.partial(program, here))
+
+    posted = board.at[: n * m - 1]
+    pltpu.make_async_copy(posted, posted, board_send).wait()
+    pltpu.make_async_copy(board, board, board_recv).wait()
+    curv_out[...] = jnp.sum(board[...], axis=0)
 
 
 def spans_of(here, batches):
@@ -534,7 +550,10 @@
     for here in range(4):
         pl.when(level == here)(functools.partial(fetch, here))
     loads[3].wait()
-    curv_small[...] = curv_buf[: curv_small.shape[0], : curv_small.shape[1]]
+    heads = curv_small.shape[1]
+    for batch in range(batches):
+        row, lane = batch * heads // 128, batch * heads % 128
+        curv_small[batch : batch + 1, :] = curv_buf[row : row + 1, lane : lane + heads]
     stores[3].start()
     for here in range(4):
         pl.when(level == here)(functools.partial(add, here))
@@ -548,7 +567,7 @@
     block = n // 4 * tokens
     rows = 16 * block
     heads = local_heads * m
-    board_shape = (-(-batch // 8) * 8, -(-heads // 128) * 128)
+    board_shape = (-(-batch * heads // 128), 128)
     result = jax.ShapeDtypeStruct(queries.shape, BF16)
     D = HEAD_DIM
     anywhere = pl.BlockSpec(memory_space=pl.ANY)
@@ -570,9 +589,7 @@
             pltpu.VMEM((16, 8, block), F32),
             pltpu.VMEM((16, 8, block), F32),
             pltpu.VMEM(board_shape, F32),
-            pltpu.VMEM((4,) + board_shape, F32),
-            pltpu.VMEM((n // 4,) + board_shape, F32),
-            pltpu.VMEM((m,) + board_shape, F32),
+            pltpu.VMEM((n * m,) + board_shape, F32),
             pltpu.SemaphoreType.DMA,
             pltpu.SemaphoreType.DMA((24,)),
             pltpu.SemaphoreType.DMA,
@@ -583,8 +600,8 @@
             pltpu.SemaphoreType.DMA((3,)),
             pltpu.SemaphoreType.DMA((3,)),
             pltpu.SemaphoreType.DMA,
-            pltpu.SemaphoreType.DMA((4,)),
-            pltpu.SemaphoreType.REGULAR,
+            pltpu.SemaphoreType.DMA,
+            pltpu.SemaphoreType.REGULAR((4,)),
         ],
         compiler_params=pltpu.CompilerParams(
             collective_id=0, has_side_effects=True, vmem_limit_bytes=56 * 1024 * 1024

time: 53.6 us -> 47.1 us (0.88)
  Pallas kernels: 52.6 us -> 46.1 us
    pallas_call x1, Pallas kernels: 50.5 us -> 44 us  [local(): pl.pallas_call(functools.partial(kernel, n, m, local_heads), out_shape=(r...]
where the time goes in v3:
time: 47.1 us; the launch traced here: 47 us
  Pallas kernels  46.1 us (98%)
  between operations  0.84 us (2%)
    pallas_call x1, Pallas kernels, local(): pl.pallas_call(functools.partial(kernel, n, m, local_heads), out_shape=(r...  44 us
    pallas_call x1, Pallas kernels, local(): pl.pallas_call(functools.partial(merge_kernel, n), out_shape=(result, res...  2.16 us

profile of v3, /device:TPU:0, one launch (start us, length us, event | category | flops | bytes accessed | tf_op | source)
XLA Modules:
  0.0 47.0 jit_solution(8993265824052108357)
XLA Ops:
  0.6 44.0 %shard_map.93 = (bf16[2,64,1024]{2,1,0:T(8,128)(2,1)}, bf16[2,64,1024]{2,1,0:T(8,128)(2,1)}, bf16[2,64,1024]{2,1,0:T(8,128)(2,1)}, bf16[2,64,1024]{2,1,0:T(8,128...) custom-call(bf16[2,64,1024]{2,1,0:T(8,128)(2,1)} %q_in.1, ...), custom_call_target="tpu_custom_call" | custom-call | tf_op jit(solution)/shard_map/pallas_call | solution.py:574
  44.6 2.2 %shard_map.94 = (bf16[2,64,1024]{2,1,0:T(8,128)(2,1)}, bf16[2,64,1024]{2,1,0:T(8,128)(2,1)}, bf16[2,64,1024]{2,1,0:T(8,128)(2,1)}, f32[2,16]{1,0:T(2,128)}) custom-call(bf16[2,64,1024]{2,1,0:T(8,128)(2,1)} %get-tuple-element.11.refs_0_, bf16[2,64,1024]{2,1,0:T(8,128)(2,1)} %get-tuple-element.12.refs_1_, bf16[2,64,1024]{2,1,0:T(8,128)(2,1)} %get-tuple-element.13.refs_2_, ...), custom_call_target="tpu_custom_call" | custom-call | tf_op jit(solution)/shard_map/pallas_call | solution.py:611

commit v4 on v3

--- a/solution.py
+++ b/solution.py
@@ -355,12 +355,12 @@
             hail(reach.at[here], below * quarter + ring, dp)
 
         if here == 0:
-            spread_all((2, K), (0, K), (3, K))
+            spread_all((2, K), (0, K), (1, K))
             relay(2, K, 1)
             relay(0, K, 2)
-            spread_all((1, K), (0, Q), (2, Q), (1, Q), (3, Q))
+            spread_all((3, K), (0, Q), (2, Q), (1, Q), (3, Q))
+            relay(1, K, 2)
             relay(3, K, 1)
-            relay(1, K, 2)
             meet()
             both_ways(0, 1, 0, 1, 1)
             whole(0, 0, 0, 1)

time: 47.1 us -> 47.2 us (level)
  no operation moved by 1% of the time
where the time goes in v4:
time: 47.2 us; the launch traced here: 47 us
  Pallas kernels  46.2 us (98%)
  between operations  0.84 us (2%)
    pallas_call x1, Pallas kernels, local(): pl.pallas_call(functools.partial(kernel, n, m, local_heads), out_shape=(r...  44 us
    pallas_call x1, Pallas kernels, local(): pl.pallas_call(functools.partial(merge_kernel, n), out_shape=(result, res...  2.16 us

profile of v4, /device:TPU:0, one launch (start us, length us, event | category | flops | bytes accessed | tf_op | source)
XLA Modules:
  0.0 47.0 jit_solution(11444810473517050692)
XLA Ops:
  0.6 44.0 %shard_map.93 = (bf16[2,64,1024]{2,1,0:T(8,128)(2,1)}, bf16[2,64,1024]{2,1,0:T(8,128)(2,1)}, bf16[2,64,1024]{2,1,0:T(8,128)(2,1)}, bf16[2,64,1024]{2,1,0:T(8,128...) custom-call(bf16[2,64,1024]{2,1,0:T(8,128)(2,1)} %q_in.1, ...), custom_call_target="tpu_custom_call" | custom-call | tf_op jit(solution)/shard_map/pallas_call | solution.py:574
  44.7 2.2 %shard_map.94 = (bf16[2,64,1024]{2,1,0:T(8,128)(2,1)}, bf16[2,64,1024]{2,1,0:T(8,128)(2,1)}, bf16[2,64,1024]{2,1,0:T(8,128)(2,1)}, f32[2,16]{1,0:T(2,128)}) custom-call(bf16[2,64,1024]{2,1,0:T(8,128)(2,1)} %get-tuple-element.11.refs_0_, bf16[2,64,1024]{2,1,0:T(8,128)(2,1)} %get-tuple-element.12.refs_1_, bf16[2,64,1024]{2,1,0:T(8,128)(2,1)} %get-tuple-element.13.refs_2_, ...), custom_call_target="tpu_custom_call" | custom-call | tf_op jit(solution)/shard_map/pallas_call | solution.py:611
